TPU v7x, 32 devices: a whole 2x2x4 slice. The times are simulated.
32 devices in a mesh: gx: 8 (over y, x, core), gy: 4 (over z).
Axes of the slice: x: 2, y: 2, z: 4, core: 2. Of those that a mesh axis runs over, the one named last changes fastest.
Arguments:
- load_cases: float32 [16, 12, 64, 128], P('gx', 'gy')
- matrix_tiles: float32 [16, 12, 64, 320], P('gx', 'gy')
- block_cols: int32 [16, 12, 5], P('gx', 'gy'), may hold values from 1 to 18, as said below
- smoother_blocks: float32 [16, 12, 4096], P('gx', 'gy')
- near_null: float32 [16, 12, 384], P('gx', 'gy'), may hold values from -0.75 to 0.75
- coarse_map: int32 [16, 12], P('gx', 'gy'), may hold values from 0 to 31, as said below
- coarse_inverse: float32 [192, 192], P(('gx', 'gy')), as said below
Outputs:
- solution: float32 [16, 12, 64, 128], P('gx', 'gy')
- residual: float32 [16, 12, 64, 128], P('gx', 'gy')
Inputs may be any that keep to these rules, and one draw needn't show every extreme that they name: `block_cols`: each aggregate's 5 slots name the aggregate itself and its four grid neighbours, each once, in an order drawn for each aggregate, as row-major indices (row width 3 + 2) into the device's block of aggregates extended by one aggregate on every side. `coarse_map`: all aggregates of one device's block of 2 x 3 aggregates map to one coarse aggregate, and different blocks to different coarse aggregates. coarse_inverse is symmetric.
All inputs are finite; a program needn't handle non-finite values.
Results may differ from a plain program's by a relative error of at most 0.0003.
Values sent between devices are 32-bit elements; how exact they have to be, the bound alone decides.
A program may use at most 64 MiB of HBM per device.

v0:
```python
import jax
import jax.numpy as jnp
from jax import lax
from jax.sharding import PartitionSpec as P

relax_weight = 0.8
highest = lax.Precision.HIGHEST


def padded(cells, sides, width):
    for axis, dim in sides:
        count = lax.axis_size(axis)
        ends = count - 1
        head = lax.slice_in_dim(cells, 0, width, axis=dim)
        tail = lax.slice_in_dim(cells, cells.shape[dim] - width, cells.shape[dim], axis=dim)
        cells = jnp.concatenate(
            [
                lax.ppermute(tail, axis, [(i, (i + 1) % count) for i in range(ends)]),
                cells,
                lax.ppermute(head, axis, [((i + 1) % count, i) for i in range(ends)]),
            ],
            axis=dim,
        )
    return cells


def per_device(
    load_cases, matrix_tiles, block_cols, smoother_blocks, near_null, coarse_map, coarse_inverse
):
    agg_rows, agg_cols, block_size, case_count = load_cases.shape
    mode_count = near_null.shape[2] // block_size
    coarse_total = coarse_inverse.shape[1]
    coarse_aggs = coarse_total // mode_count
    modes = near_null.reshape(agg_rows, agg_cols, mode_count, block_size)
    inverse_blocks = smoother_blocks.reshape(agg_rows, agg_cols, block_size, block_size)

    def operate(vector_field):
        extended = padded(vector_field, (("gx", 0), ("gy", 1)), 1)
        flattened = extended.reshape(-1, block_size, case_count)
        picked = flattened[block_cols].reshape(agg_rows, agg_cols, -1, case_count)
        return jnp.einsum("ijbk,ijkr->ijbr", matrix_tiles, picked, precision=highest)

    def smooth(defect):
        return relax_weight * jnp.einsum(
            "ijab,ijbr->ijar", inverse_blocks, defect, precision=highest
        )

    def correct(defect):
        contrib = jnp.einsum("ijkb,ijbr->ijkr", modes, defect, precision=highest)
        own_part = jnp.sum(contrib, axis=(0, 1))
        my_label = coarse_map[0, 0]
        label_value = jnp.reshape(my_label.astype(jnp.float32), (1,))
        pieces, labels = (
            lax.all_gather(own_part[None], ("gx", "gy"), axis=0, tiled=True),
            lax.all_gather(label_value, ("gx", "gy"), axis=0, tiled=True),
        )
        label_ids = labels.astype(jnp.int32)
        placing = (label_ids[:, None] == jnp.arange(coarse_aggs, dtype=jnp.int32)[None, :]).astype(
            jnp.float32
        )
        ordered = jnp.einsum("dc,dkr->ckr", placing, pieces, precision=highest).reshape(
            coarse_total, case_count
        )
        own_rows = jnp.dot(coarse_inverse, ordered, precision=highest)
        solved = lax.all_gather(own_rows, ("gx", "gy"), axis=0, tiled=True)
        mine = lax.dynamic_slice_in_dim(solved, my_label * mode_count, mode_count, 0)
        coarse_back = jnp.broadcast_to(
            mine[None, None], (agg_rows, agg_cols, mode_count, case_count)
        )
        return jnp.einsum("ijkb,ijkr->ijbr", modes, coarse_back, precision=highest)

    first = smooth(load_cases)
    first = first + correct(load_cases - operate(first))
    precond = first + smooth(load_cases - operate(first))
    defect = load_cases - operate(precond)
    update = smooth(defect)
    update = update + correct(defect - operate(update))
    update = update + smooth(defect - operate(update))
    precond = precond + update
    local_aligned = jnp.sum(load_cases * precond, axis=(0, 1, 2))
    aligned = lax.psum(local_aligned, ("gx", "gy"))
    image = operate(precond)
    curved = lax.psum(jnp.sum(precond * image, axis=(0, 1, 2)), ("gx", "gy"))
    alpha = aligned / curved
    solution = alpha * precond
    residual = load_cases - alpha * image
    return (solution, residual)


def solution(mesh):
    placed = (
        P("gx", "gy", None, None),
        P("gx", "gy", None, None),
        P("gx", "gy", None),
        P("gx", "gy", None),
        P("gx", "gy", None),
        P("gx", "gy"),
        P(("gx", "gy"), None),
    )
    return jax.shard_map(
        per_device,
        mesh=mesh,
        in_specs=placed,
        out_specs=(P("gx", "gy", None, None), P("gx", "gy", None, None)),
        check_vma=False,
    )
```

profile of v0, /device:TPU:0, one launch (start us, length us, event | category | flops | bytes accessed | tf_op | source)
XLA Modules:
  0.0 463.4 jit_solution(14982488079896245007)
XLA Ops:
  2.2 2.4 collective-permute-start
  4.6 1.3 collective-permute-start.1
  7.8 2.1 collective-permute-done.1
  9.9 3.5 collective-permute-start.2
  14.7 43.6 %all-reduce = f32[32]{0:T(128)S(1)} all-reduce(f32[32]{0:T(128)S(1)} %bitcast_dynamic-update-slice_fusion), channel_id=2, replica_groups=mesh['gx'=8,'gy'=4] {'gx','gy'}, use_global_device_ids=true, to_apply=%add | all-reduce | flops 32 | bytes 256
  61.6 66.9 %all-gather.3 = f32[32,6,128]{2,1,0:T(8,128)S(1)} all-gather(f32[1,6,128]{2,1,0:T(8,128)S(1)} %convolution_bitcast_fusion.11), channel_id=3, replica_groups=mesh['gx'=8,'gy'=4] {'gx','gy'}, dimensions={0}, use_global_device_ids=true | all-gather | bytes 101376 | tf_op jit(solution)/shard_map/all_gather | solution.py:54
  129.6 64.4 %all-gather.4 = f32[32,6,128]{2,1,0:T(8,128)S(1)} all-gather(f32[1,6,128]{2,1,0:T(8,128)S(1)} %convolution_bitcast_fusion.10), channel_id=1, replica_groups=mesh['gx'=8,'gy'=4] {'gx','gy'}, dimensions={0}, use_global_device_ids=true | all-gather | bytes 101376 | tf_op jit(solution)/shard_map/all_gather | solution.py:65
  194.6 1.3 collective-permute-start.4
  197.2 1.9 collective-permute-done.5
  199.1 4.2 collective-permute-start.6
  204.5 1.7 collective-permute-done.6
  206.3 4.1 collective-permute-done.7
  212.3 1.3 collective-permute-start.8
  214.9 4.7 %collective-permute-done.9 = f32[1,3,64,128]{3,2,1,0:T(8,128)S(1)} collective-permute-done((f32[1,3,64,128]{3,2,1,0:T(8,128)S(1)}, f32[1,3,64,128]{3,2,1,0:T(8,128)S(1)}, u32[]{:S(2)}, u32[]{:S(2)}) %collective-permute-start.9) | collective-permute-done | bytes 98336 | tf_op jit(solution)/shard_map/ppermute | solution.py:20
  219.7 1.9 collective-permute-start.10
  224.1 4.4 collective-permute-done.11
  230.4 5.0 %collective-permute-start.12 = (f32[1,3,64,128]{3,2,1,0:T(8,128)S(1)}, f32[1,3,64,128]{3,2,1,0:T(8,128)S(1)}, u32[]{:S(2)}, u32[]{:S(2)}) collective-permute-start(f32[1,3,64,128]{3,2,1,0:T(8,128)S(1)} %get-tuple-element.22), channel_id=1, source_target_pairs={{0,4},{4,8},{8,12},{12,16},{16,20},{20,24},{24,28},{1,5},{5,9},{9,... | collective-permute-start | bytes 294920 | tf_op jit(solution)/shard_map/ppermute | solution.py:18
  236.6 2.7 collective-permute-done.13
  239.4 1.9 collective-permute-start.14
  243.8 4.4 collective-permute-done.15
  250.0 64.4 %all-gather.5 = f32[32,6,128]{2,1,0:T(8,128)S(1)} all-gather(f32[1,6,128]{2,1,0:T(8,128)S(1)} %convolution_bitcast_fusion.9), channel_id=4, replica_groups=mesh['gx'=8,'gy'=4] {'gx','gy'}, dimensions={0}, use_global_device_ids=true | all-gather | bytes 101376 | tf_op jit(solution)/shard_map/all_gather | solution.py:54
  314.8 66.6 %all-gather.6 = f32[32,6,128]{2,1,0:T(8,128)S(1)} all-gather(f32[1,6,128]{2,1,0:T(8,128)S(1)} %convolution_bitcast_fusion.8), channel_id=1, replica_groups=mesh['gx'=8,'gy'=4] {'gx','gy'}, dimensions={0}, use_global_device_ids=true | all-gather | bytes 101376 | tf_op jit(solution)/shard_map/all_gather | solution.py:65
  382.0 1.3 collective-permute-start.16
  384.6 1.9 collective-permute-done.17
  386.5 1.9 collective-permute-start.18
  389.8 2.2 collective-permute-done.18
  391.9 3.4 collective-permute-done.19
  397.2 4.7 %collective-permute-start.20 = (f32[1,3,64,128]{3,2,1,0:T(8,128)S(1)}, f32[1,3,64,128]{3,2,1,0:T(8,128)S(1)}, u32[]{:S(2)}, u32[]{:S(2)}) collective-permute-start(f32[1,3,64,128]{3,2,1,0:T(8,128)S(1)} %get-tuple-element.18), channel_id=1, source_target_pairs={{0,4},{4,8},{8,12},{12,16},{16,20},{20,24},{24,28},{1,5},{5,9},{9,... | collective-permute-start | bytes 294920 | tf_op jit(solution)/shard_map/ppermute | solution.py:18
  403.2 6.4 %collective-permute-done.21 = f32[1,3,64,128]{3,2,1,0:T(8,128)S(1)} collective-permute-done((f32[1,3,64,128]{3,2,1,0:T(8,128)S(1)}, f32[1,3,64,128]{3,2,1,0:T(8,128)S(1)}, u32[]{:S(2)}, u32[]{:S(2)}) %collective-permute-start.21) | collective-permute-done | bytes 98336 | tf_op jit(solution)/shard_map/ppermute | solution.py:20
  409.7 1.9 collective-permute-start.22
  414.1 4.4 collective-permute-done.23
  420.0 42.6 %all-reduce.1 = (f32[128]{0:T(128)S(1)}, f32[128]{0:T(128)S(1)}) all-reduce(f32[128]{0:T(128)S(1)} %get-tuple-element.3, f32[128]{0:T(128)S(1)} %get-tuple-element.2), channel_id=1, replica_groups=mesh['gx'=8,'gy'=4] {'gx','gy'}, use_global_device_ids=true, to_apply=%region_1.0 | all-reduce | flops 256 | bytes 2048 | tf_op jit(solution)/shard_map/psum | solution.py:81
  (96 shorter events, 35.5 us)
Async XLA Ops:
  0.6 59.9 %copy-start = (f32[2,3,64,320]{3,2,1,0:T(8,128)S(1)}, f32[2,3,64,320]{3,2,1,0:T(8,128)}, u32[]{:S(2)}) copy-start(f32[2,3,64,320]{3,2,1,0:T(8,128)} %param.8) | copy-start | bytes 1474564
  0.6 1.2 copy-start.1
  2.2 5.6 %collective-permute-start = (f32[1,3,64,128]{3,2,1,0:T(8,128)S(1)}, f32[1,3,64,128]{3,2,1,0:T(8,128)S(1)}, u32[]{:S(2)}, u32[]{:S(2)}) collective-permute-start(f32[1,3,64,128]{3,2,1,0:T(8,128)S(1)} %get-tuple-element.28), channel_id=1, source_target_pairs={{0,4},{4,8},{8,12},{12,16},{16,20},{20,24},{24,28},{1,5},{5,9},{9,... | collective-permute-start | bytes 294920 | tf_op jit(solution)/shard_map/ppermute | solution.py:18
  4.6 5.3 %collective-permute-start.1 = (f32[1,3,64,128]{3,2,1,0:T(8,128)S(1)}, f32[1,3,64,128]{3,2,1,0:T(8,128)S(1)}, u32[]{:S(2)}, u32[]{:S(2)}) collective-permute-start(f32[1,3,64,128]{3,2,1,0:T(8,128)S(1)} %get-tuple-element.29), channel_id=1, source_target_pairs={{4,0},{8,4},{12,8},{16,12},{20,16},{24,20},{28,24},{5,1},{9,5},{13... | collective-permute-start | bytes 294920 | tf_op jit(solution)/shard_map/ppermute | solution.py:20
  5.9 0.7 copy-start.5
  9.9 4.8 %copy-start.4 = (s32[2,3,5]{2,0,1:T(2,128)S(1)}, s32[2,3,5]{2,0,1:T(2,128)}, u32[]{:S(2)}) copy-start(s32[2,3,5]{2,0,1:T(2,128)} %param.9) | copy-start | bytes 364
  9.9 49.9 %collective-permute-start.2 = (f32[4,1,64,128]{3,2,1,0:T(8,128)S(1)}, f32[4,1,64,128]{3,2,1,0:T(8,128)S(1)}, u32[]{:S(2)}, u32[]{:S(2)}) collective-permute-start(f32[4,1,64,128]{3,2,1,0:T(8,128)S(1)} %get-tuple-element.16), channel_id=1, source_target_pairs={{0,1},{1,2},{2,3},{4,5},{5,6},{6,7},{8,9},{9,10},{10,11},{12,13},{... | collective-permute-start | bytes 393224 | tf_op jit(solution)/shard_map/ppermute | solution.py:18
  13.4 46.4 %collective-permute-start.3 = (f32[4,1,64,128]{3,2,1,0:T(8,128)S(1)}, f32[4,1,64,128]{3,2,1,0:T(8,128)S(1)}, u32[]{:S(2)}, u32[]{:S(2)}) collective-permute-start(f32[4,1,64,128]{3,2,1,0:T(8,128)S(1)} %get-tuple-element.17), channel_id=1, source_target_pairs={{1,0},{2,1},{3,2},{5,4},{6,5},{7,6},{9,8},{10,9},{11,10},{13,12},{... | collective-permute-start | bytes 393224 | tf_op jit(solution)/shard_map/ppermute | solution.py:20
  59.0 0.7 copy-start.3
  128.7 0.7 copy-start.2
  194.6 2.6 collective-permute-start.4
  195.9 3.2 collective-permute-start.5
  199.1 7.2 %collective-permute-start.6 = (f32[4,1,64,128]{3,2,1,0:T(8,128)S(1)}, f32[4,1,64,128]{3,2,1,0:T(8,128)S(1)}, u32[]{:S(2)}, u32[]{:S(2)}) collective-permute-start(f32[4,1,64,128]{3,2,1,0:T(8,128)S(1)} %get-tuple-element.14), channel_id=1, source_target_pairs={{0,1},{1,2},{2,3},{4,5},{5,6},{6,7},{8,9},{9,10},{10,11},{12,13},{... | collective-permute-start | bytes 393224 | tf_op jit(solution)/shard_map/ppermute | solution.py:18
  203.2 7.2 %collective-permute-start.7 = (f32[4,1,64,128]{3,2,1,0:T(8,128)S(1)}, f32[4,1,64,128]{3,2,1,0:T(8,128)S(1)}, u32[]{:S(2)}, u32[]{:S(2)}) collective-permute-start(f32[4,1,64,128]{3,2,1,0:T(8,128)S(1)} %get-tuple-element.15), channel_id=1, source_target_pairs={{1,0},{2,1},{3,2},{5,4},{6,5},{7,6},{9,8},{10,9},{11,10},{13,12},{... | collective-permute-start | bytes 393224 | tf_op jit(solution)/shard_map/ppermute | solution.py:20
  212.3 2.6 collective-permute-start.8
  213.6 6.0 %collective-permute-start.9 = (f32[1,3,64,128]{3,2,1,0:T(8,128)S(1)}, f32[1,3,64,128]{3,2,1,0:T(8,128)S(1)}, u32[]{:S(2)}, u32[]{:S(2)}) collective-permute-start(f32[1,3,64,128]{3,2,1,0:T(8,128)S(1)} %get-tuple-element.25), channel_id=1, source_target_pairs={{4,0},{8,4},{12,8},{16,12},{20,16},{24,20},{28,24},{5,1},{9,5},{13... | collective-permute-start | bytes 294920 | tf_op jit(solution)/shard_map/ppermute | solution.py:20
  219.7 4.4 collective-permute-start.10
  221.6 6.9 %collective-permute-start.11 = (f32[4,1,64,128]{3,2,1,0:T(8,128)S(1)}, f32[4,1,64,128]{3,2,1,0:T(8,128)S(1)}, u32[]{:S(2)}, u32[]{:S(2)}) collective-permute-start(f32[4,1,64,128]{3,2,1,0:T(8,128)S(1)} %get-tuple-element.13), channel_id=1, source_target_pairs={{1,0},{2,1},{3,2},{5,4},{6,5},{7,6},{9,8},{10,9},{11,10},{13,12},{... | collective-permute-start | bytes 393224 | tf_op jit(solution)/shard_map/ppermute | solution.py:20
  230.4 6.3 %collective-permute-start.12 = (f32[1,3,64,128]{3,2,1,0:T(8,128)S(1)}, f32[1,3,64,128]{3,2,1,0:T(8,128)S(1)}, u32[]{:S(2)}, u32[]{:S(2)}) collective-permute-start(f32[1,3,64,128]{3,2,1,0:T(8,128)S(1)} %get-tuple-element.22), channel_id=1, source_target_pairs={{0,4},{4,8},{8,12},{12,16},{16,20},{20,24},{24,28},{1,5},{5,9},{9,... | collective-permute-start | bytes 294920 | tf_op jit(solution)/shard_map/ppermute | solution.py:18
  235.3 4.0 collective-permute-start.13
  239.4 4.4 collective-permute-start.14
  241.3 6.9 %collective-permute-start.15 = (f32[4,1,64,128]{3,2,1,0:T(8,128)S(1)}, f32[4,1,64,128]{3,2,1,0:T(8,128)S(1)}, u32[]{:S(2)}, u32[]{:S(2)}) collective-permute-start(f32[4,1,64,128]{3,2,1,0:T(8,128)S(1)} %get-tuple-element.11), channel_id=1, source_target_pairs={{1,0},{2,1},{3,2},{5,4},{6,5},{7,6},{9,8},{10,9},{11,10},{13,12},{... | collective-permute-start | bytes 393224 | tf_op jit(solution)/shard_map/ppermute | solution.py:20
  382.0 2.6 collective-permute-start.16
  383.3 3.2 collective-permute-start.17
  386.5 5.4 %collective-permute-start.18 = (f32[4,1,64,128]{3,2,1,0:T(8,128)S(1)}, f32[4,1,64,128]{3,2,1,0:T(8,128)S(1)}, u32[]{:S(2)}, u32[]{:S(2)}) collective-permute-start(f32[4,1,64,128]{3,2,1,0:T(8,128)S(1)} %get-tuple-element.8), channel_id=1, source_target_pairs={{0,1},{1,2},{2,3},{4,5},{5,6},{6,7},{8,9},{9,10},{10,11},{12,13},{... | collective-permute-start | bytes 393224 | tf_op jit(solution)/shard_map/ppermute | solution.py:18
  388.5 6.9 %collective-permute-start.19 = (f32[4,1,64,128]{3,2,1,0:T(8,128)S(1)}, f32[4,1,64,128]{3,2,1,0:T(8,128)S(1)}, u32[]{:S(2)}, u32[]{:S(2)}) collective-permute-start(f32[4,1,64,128]{3,2,1,0:T(8,128)S(1)} %get-tuple-element.9), channel_id=1, source_target_pairs={{1,0},{2,1},{3,2},{5,4},{6,5},{7,6},{9,8},{10,9},{11,10},{13,12},{... | collective-permute-start | bytes 393224 | tf_op jit(solution)/shard_map/ppermute | solution.py:20
  397.2 6.0 %collective-permute-start.20 = (f32[1,3,64,128]{3,2,1,0:T(8,128)S(1)}, f32[1,3,64,128]{3,2,1,0:T(8,128)S(1)}, u32[]{:S(2)}, u32[]{:S(2)}) collective-permute-start(f32[1,3,64,128]{3,2,1,0:T(8,128)S(1)} %get-tuple-element.18), channel_id=1, source_target_pairs={{0,4},{4,8},{8,12},{12,16},{16,20},{20,24},{24,28},{1,5},{5,9},{9,... | collective-permute-start | bytes 294920 | tf_op jit(solution)/shard_map/ppermute | solution.py:18
  401.9 7.7 %collective-permute-start.21 = (f32[1,3,64,128]{3,2,1,0:T(8,128)S(1)}, f32[1,3,64,128]{3,2,1,0:T(8,128)S(1)}, u32[]{:S(2)}, u32[]{:S(2)}) collective-permute-start(f32[1,3,64,128]{3,2,1,0:T(8,128)S(1)} %get-tuple-element.19), channel_id=1, source_target_pairs={{4,0},{8,4},{12,8},{16,12},{20,16},{24,20},{28,24},{5,1},{9,5},{13... | collective-permute-start | bytes 294920 | tf_op jit(solution)/shard_map/ppermute | solution.py:20
  409.7 4.4 collective-permute-start.22
  411.6 6.9 %collective-permute-start.23 = (f32[4,1,64,128]{3,2,1,0:T(8,128)S(1)}, f32[4,1,64,128]{3,2,1,0:T(8,128)S(1)}, u32[]{:S(2)}, u32[]{:S(2)}) collective-permute-start(f32[4,1,64,128]{3,2,1,0:T(8,128)S(1)} %get-tuple-element.7), channel_id=1, source_target_pairs={{1,0},{2,1},{3,2},{5,4},{6,5},{7,6},{9,8},{10,9},{11,10},{13,12},{... | collective-permute-start | bytes 393224 | tf_op jit(solution)/shard_map/ppermute | solution.py:20
where the time goes:
time: 464 us; the launch traced here: 463 us
  blocking collectives  348 us (75%)
  waiting for transfers between devices  47.9 us (10%)
  starting transfers between devices  46.8 us (10%)
  matrix products  8.68 us (2%)
  local copies, waits for them, and re-layouts  7.77 us (2%)
    all_gather x2, blocking collectives, correct(): lax.all_gather(own_part[None], ('gx', 'gy'), axis=0, tiled=True)  131 us
    all_gather x2, blocking collectives, correct(): solved = lax.all_gather(own_rows, ('gx', 'gy'), axis=0, tiled=True)  131 us
    unnamed x1, blocking collectives  43.6 us
    psum x1, blocking collectives, per_device(): aligned = lax.psum(local_aligned, ('gx', 'gy'))  42.6 us
    ppermute x12, waiting for transfers between devices, padded(): lax.ppermute(head, axis, [((i + 1) % count, i) for i in range(ends)])  40.3 us
    ppermute x12, starting transfers between devices, padded(): lax.ppermute(tail, axis, [(i, (i + 1) % count) for i in range(ends)])  31.3 us
    ppermute x12, starting transfers between devices, padded(): lax.ppermute(head, axis, [((i + 1) % count, i) for i in range(ends)])  15.5 us
  transfers between devices with their start and end apart: 24, of which 16 were waited for; matrix products, arithmetic and copies ran while one was open for 0% of the time, Pallas kernels for 0%

commit v1 on v0

--- a/solution.py
+++ b/solution.py
@@ -1,6 +1,10 @@
+import functools
+
 import jax
 import jax.numpy as jnp
 from jax import lax
+from jax.experimental import pallas as pl
+from jax.experimental.pallas import tpu as pltpu
 from jax.sharding import PartitionSpec as P
 
 relax_weight = 0.8
@@ -22,6 +26,366 @@
             axis=dim,
         )
     return cells
+
+
+def cut(v):
+    hi = v.astype(jnp.bfloat16)
+    return hi, (v - hi.astype(jnp.float32)).astype(jnp.bfloat16)
+
+
+def stacked(v):
+    hi, lo = cut(v)
+    return jnp.concatenate([hi, lo, hi], axis=0)
+
+
+def mm(a, b):
+    return lax.dot_general(a, b, (((1,), (0,)), ((), ())), preferred_element_type=jnp.float32)
+
+
+def mm_t(a, b, precision=None):
+    return lax.dot_general(
+        a, b, (((1,), (1,)), ((), ())), precision=precision, preferred_element_type=jnp.float32
+    )
+
+
+def mm3(a_cut, b):
+    hi, lo = cut(b)
+    return mm(a_cut[0], hi) + (mm(a_cut[0], lo) + mm(a_cut[1], hi))
+
+
+def step_kernel(
+    nx, ny, modes,
+    b_ref, a_ref, cols_ref, s_ref, n_ref, map_ref, inv_ref,
+    sol_ref, res_ref,
+    field, up, down, left, right, local, edge, smoother, info, info_all, near, coarse, coarse_all,
+    sums, sums_all, halo_send, halo_recv, near_send, near_recv, all_send, all_recv,
+):
+    rows, cols, blk, cases = b_ref.shape
+    count = rows * cols
+    size = count * blk
+    n = nx * ny
+    width = info.shape[1]
+    coarse_rows = n * 8
+    x, y = lax.axis_index("gx"), lax.axis_index("gy")
+    me = x * ny + y
+    sides = (
+        (x > 0, (x - 1, y)),
+        (x < nx - 1, (x + 1, y)),
+        (y > 0, (x, y - 1)),
+        (y < ny - 1, (x, y + 1)),
+    )
+    halos = (up, down, left, right)
+
+    barrier = pltpu.get_barrier_semaphore()
+
+    def greet(j, carry):
+        peer = lax.rem(me + j, n)
+        pl.semaphore_signal(
+            barrier, inc=1, device_id=(peer // ny, lax.rem(peer, ny)),
+            device_id_type=pl.DeviceIdType.MESH,
+        )
+        return carry
+
+    lax.fori_loop(1, n, greet, 0)
+
+    def send_all(src, dst, k):
+        def one(j, carry):
+            peer = lax.rem(me + j, n)
+            pltpu.make_async_remote_copy(
+                src_ref=src, dst_ref=dst.at[me],
+                send_sem=all_send.at[k], recv_sem=all_recv.at[k],
+                device_id=(peer // ny, lax.rem(peer, ny)),
+                device_id_type=pl.DeviceIdType.MESH,
+            ).start()
+            return carry
+
+        lax.fori_loop(1, n, one, 0)
+
+    def wait_all(dst, sem):
+        others = dst.at[pl.ds(0, n - 1)]
+        pltpu.make_async_copy(others, others, sem).wait()
+
+    def halo_copies(k):
+        now = field.at[k]
+        out = (
+            (now.at[0], down.at[k], 1),
+            (now.at[rows - 1], up.at[k], 0),
+            (now.at[:, 0], right.at[k], 3),
+            (now.at[:, cols - 1], left.at[k], 2),
+        )
+        return [
+            pltpu.make_async_remote_copy(
+                src_ref=src, dst_ref=dst,
+                send_sem=halo_send.at[k, side], recv_sem=halo_recv.at[k, lands],
+                device_id=peer, device_id_type=pl.DeviceIdType.MESH,
+            )
+            for side, ((src, dst, lands), (_, peer)) in enumerate(zip(out, sides))
+        ]
+
+    def halo_start(k):
+        for (here, _), copy in zip(sides, halo_copies(k)):
+            pl.when(here)(copy.start)
+
+    def halo_wait(k):
+        for side, (here, _) in enumerate(sides):
+            buf = halos[side].at[k]
+            pl.when(here)(pltpu.make_async_copy(buf, buf, halo_recv.at[k, side]).wait)
+
+    def near_copies():
+        return [
+            pltpu.make_async_remote_copy(
+                src_ref=n_ref, dst_ref=near.at[lands],
+                send_sem=near_send.at[side], recv_sem=near_recv.at[lands],
+                device_id=peer, device_id_type=pl.DeviceIdType.MESH,
+            )
+            for side, (lands, (_, peer)) in enumerate(zip((1, 0, 3, 2), sides))
+        ]
+
+    for p in range(count):
+        hi, lo = cut(relax_weight * s_ref[p])
+        smoother[p] = jnp.concatenate([hi, hi, lo], axis=1)
+
+    def smooth(v):
+        return jnp.concatenate(
+            [mm(smoother[p], stacked(v[p * blk : (p + 1) * blk])) for p in range(count)], axis=0
+        )
+
+    b = b_ref[...].reshape(size, cases)
+    first = smooth(b)
+    field[0] = first.reshape(rows, cols, blk, cases)
+    for side, (here, _) in enumerate(sides):
+
+        @pl.when(jnp.logical_not(here))
+        def _():
+            halos[side][...] = jnp.zeros_like(halos[side])
+            near[side] = jnp.zeros_like(near[side])
+
+    info[...] = jnp.zeros_like(info)
+    info[0:modes, 0 : inv_ref.shape[1]] = inv_ref[...]
+    info[modes : modes + 1, :] = jnp.full((1, width), map_ref[0, 0].astype(jnp.float32))
+
+    pl.semaphore_wait(barrier, n - 1)
+    halo_start(0)
+    for (here, _), copy in zip(sides, near_copies()):
+        pl.when(here)(copy.start)
+    send_all(info, info_all, 0)
+    info_all[pl.ds(me, 1)] = info[...][None]
+
+    local[...] = jnp.zeros_like(local)
+    for i in range(rows):
+        for j in range(cols):
+            p = i * cols + j
+            tiles = [a_ref[i, j, :, s * blk : (s + 1) * blk] for s in range(5)]
+            names = [cols_ref[i, j, s] for s in range(5)]
+            for d, (di, dj) in enumerate(((0, 0), (-1, 0), (1, 0), (0, -1), (0, 1))):
+                e = (i + 1 + di) * (cols + 2) + j + 1 + dj
+                tile = tiles[0] * (names[0] == e).astype(jnp.float32)
+                for s in range(1, 5):
+                    tile = tile + tiles[s] * (names[s] == e).astype(jnp.float32)
+                hi, lo = cut(tile)
+                ii, jj = i + di, j + dj
+                if 0 <= ii < rows and 0 <= jj < cols:
+                    q = ii * cols + jj
+                    for k, part in enumerate((hi, hi, lo)):
+                        at = k * size + q * blk
+                        local[p * blk : (p + 1) * blk, at : at + blk] = part
+                else:
+                    at = (0, j, cols + j, 2 * cols + i, 2 * cols + rows + i)[d]
+                    edge[at] = jnp.concatenate([hi, hi, lo], axis=1)
+
+    def places():
+        for j in range(cols):
+            yield 0, j, j, j
+        for j in range(cols):
+            yield 1, j, cols + j, (rows - 1) * cols + j
+        for i in range(rows):
+            yield 2, i, 2 * cols + i, i * cols
+        for i in range(rows):
+            yield 3, i, 2 * cols + rows + i, i * cols + cols - 1
+
+    def operate(v, k):
+        inner = mm(local[...], stacked(v))
+        parts = [inner[p * blk : (p + 1) * blk] for p in range(count)]
+        halo_wait(k)
+        for side, at, e, p in places():
+            parts[p] = parts[p] + mm(edge[e], stacked(halos[side][k, at]))
+        return jnp.concatenate(parts, axis=0)
+
+    own_n = n_ref[...]
+    own_hi, own_lo = cut(own_n)
+    own_cat = jnp.concatenate([own_hi, own_hi, own_lo], axis=1)
+
+    def restrict(v, k):
+        g = mm(own_cat, stacked(v))
+        coarse[k] = g
+        send_all(coarse.at[k], coarse_all.at[k], 1 + k)
+        coarse_all[k, pl.ds(me, 1)] = g[None]
+
+    r = b - operate(first, 0)
+    restrict(r, 0)
+
+    for side, (here, _) in enumerate(sides):
+        buf = near.at[side]
+        pl.when(here)(pltpu.make_async_copy(buf, buf, near_recv.at[side]).wait)
+
+    def at_rows(t, v):
+        pieces = [jnp.zeros_like(v)] * 6
+        pieces[t] = v
+        return jnp.concatenate(pieces, axis=0)
+
+    def across(v):
+        hi, lo = cut(v)
+        return jnp.concatenate([hi, lo, hi], axis=1)
+
+    spread = mm_t(local[...], across(at_rows(0, own_n)))
+    parts = [spread[p * blk : (p + 1) * blk] for p in range(count)]
+    theirs = [near[side] for side in range(4)]
+    facing = (
+        lambda at: (rows - 1) * cols + at,
+        lambda at: at,
+        lambda at: at * cols + cols - 1,
+        lambda at: at * cols,
+    )
+    for side, at, e, p in places():
+        q = facing[side](at)
+        block = theirs[side][:, q * blk : (q + 1) * blk]
+        parts[p] = parts[p] + mm_t(edge[e], across(at_rows(1 + side, block)))
+    spread_cut = cut(jnp.concatenate(parts, axis=0))
+    eye = (
+        lax.broadcasted_iota(jnp.int32, (size, size), 0)
+        == lax.broadcasted_iota(jnp.int32, (size, size), 1)
+    ).astype(jnp.float32).astype(jnp.bfloat16)
+    prolong_cut = tuple(
+        mm_t(eye, part).astype(jnp.bfloat16) for part in cut(at_rows(0, own_n))
+    )
+
+    wait_all(info_all, all_recv.at[0])
+    inv_all = info_all[...].reshape(coarse_rows, width)
+    ids = [me] + [
+        jnp.clip(px, 0, nx - 1) * ny + jnp.clip(py, 0, ny - 1) for _, (px, py) in sides
+    ]
+    lane = lax.broadcasted_iota(jnp.int32, (8, coarse_rows), 1)
+    row = lax.broadcasted_iota(jnp.int32, (8, coarse_rows), 0)
+    pick = []
+    for d in ids:
+        tile = info_all[pl.ds(d, 1)].reshape(8, width)
+        label = jnp.broadcast_to(tile[modes : modes + 1, 0:1], (8, coarse_rows))
+        wanted = label * 8.0 + row.astype(jnp.float32)
+        hit = jnp.where(lane.astype(jnp.float32) == wanted, 1.0, 0.0)
+        pick.append(jnp.where(row < modes, hit, 0.0))
+    pick.append(jnp.zeros((8, coarse_rows), jnp.float32))
+    picked = lax.dot_general(
+        jnp.concatenate(pick, axis=0), inv_all, (((1,), (0,)), ((), ())),
+        precision=highest, preferred_element_type=jnp.float32,
+    )
+    lane3 = lax.broadcasted_iota(jnp.int32, (n, 8, width), 2).astype(jnp.float32)
+    row3 = lax.broadcasted_iota(jnp.int32, (n, 8, width), 1)
+    labels = jnp.broadcast_to(info_all[...][:, modes : modes + 1, :], (n, 8, width))
+    order = jnp.where(lane3 == labels * float(modes) + row3.astype(jnp.float32), 1.0, 0.0)
+    order = jnp.where(row3 < modes, order, 0.0).reshape(coarse_rows, width)
+    solve_cut = cut(mm_t(picked, order, precision=highest))
+
+    def correct(k):
+        wait_all(coarse_all.at[k], all_recv.at[1 + k])
+        h = mm3(solve_cut, coarse_all[k].reshape(coarse_rows, cases))
+        return mm3(prolong_cut, h), mm3(spread_cut, h)
+
+    def relax(v, k):
+        s = smooth(v)
+        field[k] = s.reshape(rows, cols, blk, cases)
+        halo_start(k)
+        return s, v - operate(s, k)
+
+    up_by, down_by = correct(0)
+    precond = first + up_by
+    r = r - down_by
+    s, r = relax(r, 1)
+    precond = precond + s
+    s, r = relax(r, 2)
+    precond = precond + s
+    restrict(r, 1)
+    up_by, down_by = correct(1)
+    precond = precond + up_by
+    r = r - down_by
+    s, r = relax(r, 3)
+    precond = precond + s
+
+    image = b - r
+    sums[...] = jnp.concatenate(
+        [
+            jnp.sum(b * precond, axis=0, keepdims=True),
+            jnp.sum(precond * image, axis=0, keepdims=True),
+            jnp.zeros((6, cases), jnp.float32),
+        ],
+        axis=0,
+    )
+    send_all(sums, sums_all, 3)
+    sums_all[pl.ds(me, 1)] = sums[...][None]
+    wait_all(sums_all, all_recv.at[3])
+    total = jnp.sum(sums_all[...], axis=0)
+    alpha = total[0:1] / total[1:2]
+    sol_ref[...] = (alpha * precond).reshape(rows, cols, blk, cases)
+    res_ref[...] = (b - alpha * image).reshape(rows, cols, blk, cases)
+
+    for k in range(4):
+        for (here, _), copy in zip(sides, halo_copies(k)):
+            pl.when(here)(copy.wait_send)
+    for (here, _), copy in zip(sides, near_copies()):
+        pl.when(here)(copy.wait_send)
+    wait_all(info_all, all_send.at[0])
+    wait_all(coarse_all.at[0], all_send.at[1])
+    wait_all(coarse_all.at[1], all_send.at[2])
+    wait_all(sums_all, all_send.at[3])
+
+
+def fused(
+    nx, ny,
+    load_cases, matrix_tiles, block_cols, smoother_blocks, near_null, coarse_map, coarse_inverse
+):
+    rows, cols, blk, cases = load_cases.shape
+    count = rows * cols
+    modes = near_null.shape[2] // blk
+    n = nx * ny
+    width = -(-coarse_inverse.shape[1] // 128) * 128
+    near = jnp.transpose(near_null.reshape(count, modes, blk), (1, 0, 2)).reshape(modes, -1)
+    near = jnp.pad(near, ((0, 8 - modes), (0, 0)))
+    blocks = smoother_blocks.reshape(count, blk, blk)
+    vmem = pl.BlockSpec(memory_space=pltpu.VMEM)
+    smem = pl.BlockSpec(memory_space=pltpu.SMEM)
+    f32, bf16 = jnp.float32, jnp.bfloat16
+    shape = jax.ShapeDtypeStruct(load_cases.shape, f32)
+    return pl.pallas_call(
+        functools.partial(step_kernel, nx, ny, modes),
+        out_shape=(shape, shape),
+        in_specs=[vmem, vmem, smem, vmem, vmem, smem, vmem],
+        out_specs=(vmem, vmem),
+        scratch_shapes=[
+            pltpu.VMEM((4, rows, cols, blk, cases), f32),
+            pltpu.VMEM((4, cols, blk, cases), f32),
+            pltpu.VMEM((4, cols, blk, cases), f32),
+            pltpu.VMEM((4, rows, blk, cases), f32),
+            pltpu.VMEM((4, rows, blk, cases), f32),
+            pltpu.VMEM((count * blk, 3 * count * blk), bf16),
+            pltpu.VMEM((2 * (rows + cols), blk, 3 * blk), bf16),
+            pltpu.VMEM((count, blk, 3 * blk), bf16),
+            pltpu.VMEM((8, width), f32),
+            pltpu.VMEM((n, 8, width), f32),
+            pltpu.VMEM((4, 8, count * blk), f32),
+            pltpu.VMEM((2, 8, cases), f32),
+            pltpu.VMEM((2, n, 8, cases), f32),
+            pltpu.VMEM((8, cases), f32),
+            pltpu.VMEM((n, 8, cases), f32),
+            pltpu.SemaphoreType.DMA((4, 4)),
+            pltpu.SemaphoreType.DMA((4, 4)),
+            pltpu.SemaphoreType.DMA((4,)),
+            pltpu.SemaphoreType.DMA((4,)),
+            pltpu.SemaphoreType.DMA((4,)),
+            pltpu.SemaphoreType.DMA((4,)),
+        ],
+        compiler_params=pltpu.CompilerParams(
+            collective_id=0, has_side_effects=True, vmem_limit_bytes=60 * 2**20
+        ),
+    )(load_cases, matrix_tiles, block_cols, blocks, near, coarse_map, coarse_inverse)
 
 
 def per_device(
@@ -88,6 +452,8 @@
 
 
 def solution(mesh):
+    nx, ny = mesh.shape["gx"], mesh.shape["gy"]
+    step = functools.partial(fused, nx, ny) if nx * ny <= 128 else per_device
     placed = (
         P("gx", "gy", None, None),
         P("gx", "gy", None, None),
@@ -98,7 +464,7 @@
         P(("gx", "gy"), None),
     )
     return jax.shard_map(
-        per_device,
+        step,
         mesh=mesh,
         in_specs=placed,
         out_specs=(P("gx", "gy", None, None), P("gx", "gy", None, None)),

time: 464 us -> 53.6 us (0.12)
  blocking collectives: 348 us -> 0 us
  waiting for transfers between devices: 47.9 us -> 0 us
  starting transfers between devices: 46.8 us -> 0 us
  Pallas kernels: 0 us -> 46.6 us
  matrix products: 8.68 us -> 0 us
    all_gather x4 -> x0, blocking collectives: 262 us -> none  [the longest x2 131 us: correct(): lax.all_gather(own_part[None], ('gx', 'gy'), axis=0, tiled=True)]
    ppermute x24 -> x0, waiting for transfers between devices: 47.9 us -> none  [the longest x12 40.3 us: padded(): lax.ppermute(head, axis, [((i + 1) % count, i) for i in range(ends)])]
    ppermute x24 -> x0, starting transfers between devices: 46.8 us -> none  [the longest x12 31.3 us: padded(): lax.ppermute(tail, axis, [(i, (i + 1) % count) for i in range(ends)])]
    pallas_call x0 -> x1, Pallas kernels: none -> 46.6 us  [fused(): pl.pallas_call(functools.partial(step_kernel, nx, ny, modes), out_shape=(...]
    unnamed x1 -> x0, blocking collectives: 43.6 us -> none
    psum x1 -> x0, blocking collectives: 42.6 us -> none  [per_device(): aligned = lax.psum(local_aligned, ('gx', 'gy'))]
    dot_general x18 -> x0, matrix products: 8.68 us -> none  [the longest x6 5.2 us: operate(): jnp.einsum('ijbk,ijkr->ijbr', matrix_tiles, picked, precision=highest)]
  transfers between devices with their start and end apart: 24 -> 0, of which waited for: 16 -> 0; matrix products, arithmetic and copies ran while one was open for 0% -> 0% of each run, Pallas kernels for 0% -> 0%
where the time goes in v1:
time: 53.6 us; the launch traced here: 53.3 us
  Pallas kernels  46.6 us (87%)
  local copies, waits for them, and re-layouts  6.04 us (11%)
  between operations  0.66 us (1%)
    pallas_call x1, Pallas kernels, fused(): pl.pallas_call(functools.partial(step_kernel, nx, ny, modes), out_shape=(...  46.6 us
    unnamed x9, local copies, waits for them, and re-layouts  4.43 us

profile of v1, /device:TPU:0, one launch (start us, length us, event | category | flops | bytes accessed | tf_op | source)
XLA Modules:
  0.0 53.3 jit_solution(3346735159988369926)
XLA Ops:
  0.6 0.0 copy-start.1
  0.6 1.3 %copy.14.cols_ref = s32[2,3,5]{2,1,0:T(4,128)} copy(s32[2,3,5]{2,0,1:T(2,128)} %param.9) | data formatting | bytes 240 | tf_op args[2]
  2.0 0.7 %copy.12 = f32[2,3,384]{2,1,0:T(4,128)S(1)} copy(f32[2,3,384]{2,0,1:T(2,128)} %param.11) | data formatting | bytes 18432 | tf_op args[4]
  2.7 0.1 reshape.14
  2.8 0.1 reshape.15
  2.8 0.6 %pad.4.n_ref = f32[8,384]{1,0:T(8,128)} pad(f32[6,384]{1,0:T(8,128)S(1)} %reshape.15, f32[]{:T(128)} %constant.2.clone.1), padding=0_2x0_0 | pad | bytes 21508 | tf_op jit(solution)/shard_map/jit(_pad)/pad | solution.py:351
  3.4 0.0 copy-done.1
  3.4 0.1 copy.11
  3.5 0.8 %reshape.13.s_ref = f32[6,64,64]{2,1,0:T(8,128)} reshape(f32[2,3,4096]{2,1,0:T(4,128)S(1)} %copy.11) | data formatting | bytes 196608 | tf_op jit(solution)/shard_map/reshape | solution.py:352
  4.3 46.6 %shard_map.86 = (f32[2,3,64,128]{3,2,1,0:T(8,128)}, f32[2,3,64,128]{3,2,1,0:T(8,128)}) custom-call(f32[2,3,64,128]{3,2,1,0:T(8,128)} %b_ref.1, f32[2,3,64,320]{3,2,1,0:T(8,128)} %a_ref.1, s32[2,3,5]{2,1,0:T(4,128)} %copy.14.cols_ref, f32[6,64,64]{2,1,0:T(8,128)} %reshape.13.s_ref, f32[8,384]{1,0:T(8,128)} %pad.4.n_ref, s32[2,3]{1,0:T(2,128)} %map_ref.1, ...), custom_call_target="tpu_custom_call" | custom-call | tf_op jit(solution)/shard_map/pallas_call | solution.py:357
  51.0 0.0 copy-start
  51.0 1.7 %copy.17 = f32[2,3,64,128]{3,2,1,0:T(8,128)} copy(f32[2,3,64,128]{3,2,1,0:T(8,128)} %get-tuple-element.4) | data formatting | bytes 393216
  52.6 0.0 copy-done
  52.6 0.7 %copy.18 = f32[2,3,64,128]{3,2,1,0:T(8,128)} copy(f32[2,3,64,128]{3,2,1,0:T(8,128)S(1)} %copy-done) | data formatting | bytes 393216
  (1 shorter events, 0.0 us)
Async XLA Ops:
  0.6 2.8 %copy-start.1 = (f32[2,3,4096]{2,0,1:T(2,128)S(1)}, f32[2,3,4096]{2,0,1:T(2,128)}, u32[]{:S(2)}) copy-start(f32[2,3,4096]{2,0,1:T(2,128)} %param.10) | copy-start | bytes 294916
  51.0 1.7 %copy-start = (f32[2,3,64,128]{3,2,1,0:T(8,128)S(1)}, f32[2,3,64,128]{3,2,1,0:T(8,128)}, u32[]{:S(2)}) copy-start(f32[2,3,64,128]{3,2,1,0:T(8,128)} %get-tuple-element.5) | copy-start | bytes 589828

commit v2 on v1

--- a/solution.py
+++ b/solution.py
@@ -55,10 +55,12 @@
 
 def step_kernel(
     nx, ny, modes,
-    b_ref, a_ref, cols_ref, s_ref, n_ref, map_ref, inv_ref,
-    sol_ref, res_ref,
-    field, up, down, left, right, local, edge, smoother, info, info_all, near, coarse, coarse_all,
-    sums, sums_all, halo_send, halo_recv, near_send, near_recv, all_send, all_recv,
+    b_hbm, a_hbm, cols_hbm, s_hbm, n_hbm, map_hbm, inv_hbm,
+    precond_ref, image_ref, alpha_ref,
+    b_ref, a_ref, cols_ref, s_ref, n_ref, map_ref, inv_ref, loaded,
+    blocks, nulls, field, up, down, left, right, local, edge, smoother, info, info_all, near, coarse, coarse_all,
+    sums, sums_all, halo_send, halo_recv, near_send, near_recv, col_send, col_recv,
+    all_send, all_recv, sum_send, sum_recv,
 ):
     rows, cols, blk, cases = b_ref.shape
     count = rows * cols
@@ -76,6 +78,7 @@
     )
     halos = (up, down, left, right)
 
+    coarse_all[...] = jnp.zeros_like(coarse_all)
     barrier = pltpu.get_barrier_semaphore()
 
     def greet(j, carry):
@@ -88,22 +91,62 @@
 
     lax.fori_loop(1, n, greet, 0)
 
-    def send_all(src, dst, k):
+    loads = [
+        pltpu.make_async_copy(src, dst, loaded.at[i])
+        for i, (src, dst) in enumerate(
+            (
+                (s_hbm, s_ref), (b_hbm, b_ref), (n_hbm, n_ref), (inv_hbm, inv_ref),
+                (map_hbm, map_ref), (cols_hbm, cols_ref), (a_hbm, a_ref),
+            )
+        )
+    ]
+    for load in loads:
+        load.start()
+
+    def at_column(src, dst, k):
+        copies = []
+        for j in range(1, ny):
+            copies.append(
+                pltpu.make_async_remote_copy(
+                    src_ref=src, dst_ref=dst.at[me], send_sem=col_send.at[k, j],
+                    recv_sem=col_recv.at[k, ny - j],
+                    device_id=(x, lax.rem(y + j, ny)), device_id_type=pl.DeviceIdType.MESH,
+                )
+            )
+        return copies
+
+    def pass_on(src, dst, slot, k):
         def one(j, carry):
-            peer = lax.rem(me + j, n)
             pltpu.make_async_remote_copy(
-                src_ref=src, dst_ref=dst.at[me],
-                send_sem=all_send.at[k], recv_sem=all_recv.at[k],
-                device_id=(peer // ny, lax.rem(peer, ny)),
-                device_id_type=pl.DeviceIdType.MESH,
+                src_ref=src, dst_ref=dst.at[slot], send_sem=all_send.at[k], recv_sem=all_recv.at[k],
+                device_id=(lax.rem(x + j, nx), y), device_id_type=pl.DeviceIdType.MESH,
             ).start()
             return carry
 
-        lax.fori_loop(1, n, one, 0)
-
-    def wait_all(dst, sem):
-        others = dst.at[pl.ds(0, n - 1)]
-        pltpu.make_async_copy(others, others, sem).wait()
+        lax.fori_loop(1, nx, one, 0)
+
+    def gather_start(src, dst, k):
+        for copy in at_column(src, dst, k):
+            copy.start()
+        pass_on(src, dst, me, k)
+
+    def gather_pass(src, dst, k):
+        for j in list(range(1, ny, 2)) + list(range(2, ny, 2)):
+            slot = x * ny + lax.rem(y + j, ny)
+            pltpu.make_async_copy(src, src, col_recv.at[k, j]).wait()
+            pass_on(dst.at[slot], dst, slot, k)
+
+    def wait_many(dst, tiles, sem):
+        some = dst.at[pl.ds(0, tiles)]
+        pltpu.make_async_copy(some, some, sem).wait()
+
+    def gather_end(dst, k):
+        wait_many(dst, (nx - 1) * ny, all_recv.at[k])
+
+    def gather_sent(src, dst, k):
+        for copy in at_column(src, dst, k):
+            copy.wait_send()
+        wait_many(dst, (nx - 1) * ny, all_send.at[k])
 
     def halo_copies(k):
         now = field.at[k]
@@ -134,15 +177,26 @@
     def near_copies():
         return [
             pltpu.make_async_remote_copy(
-                src_ref=n_ref, dst_ref=near.at[lands],
+                src_ref=nulls, dst_ref=near.at[lands],
                 send_sem=near_send.at[side], recv_sem=near_recv.at[lands],
                 device_id=peer, device_id_type=pl.DeviceIdType.MESH,
             )
             for side, (lands, (_, peer)) in enumerate(zip((1, 0, 3, 2), sides))
         ]
 
+    loads[0].wait()
+    for i in range(rows):
+        for j in range(cols):
+            p = i * cols + j
+            for c in range(0, blk * blk, 128):
+                blocks[p, 0, c // 128 : c // 128 + 1] = s_ref[j, i : i + 1, c : c + 128]
+            flat = blocks[p, 0, 0 : blk * blk // 128]
+            for half in range(128 // blk):
+                blocks[p, 1, pl.ds(half, blk * blk // 128, stride=128 // blk), 0:blk] = flat[
+                    :, half * blk : (half + 1) * blk
+                ]
     for p in range(count):
-        hi, lo = cut(relax_weight * s_ref[p])
+        hi, lo = cut(relax_weight * blocks[p, 1, :, 0:blk])
         smoother[p] = jnp.concatenate([hi, hi, lo], axis=1)
 
     def smooth(v):
@@ -150,6 +204,7 @@
             [mm(smoother[p], stacked(v[p * blk : (p + 1) * blk])) for p in range(count)], axis=0
         )
 
+    loads[1].wait()
     b = b_ref[...].reshape(size, cases)
     first = smooth(b)
     field[0] = first.reshape(rows, cols, blk, cases)
@@ -160,6 +215,16 @@
             halos[side][...] = jnp.zeros_like(halos[side])
             near[side] = jnp.zeros_like(near[side])
 
+    for load in loads[2:5]:
+        load.wait()
+    nulls[...] = jnp.zeros_like(nulls)
+    for i in range(rows):
+        for j in range(cols):
+            p = i * cols + j
+            for k in range(modes):
+                nulls[k : k + 1, p * blk : (p + 1) * blk] = n_ref[
+                    j, i : i + 1, k * blk : (k + 1) * blk
+                ]
     info[...] = jnp.zeros_like(info)
     info[0:modes, 0 : inv_ref.shape[1]] = inv_ref[...]
     info[modes : modes + 1, :] = jnp.full((1, width), map_ref[0, 0].astype(jnp.float32))
@@ -168,15 +233,17 @@
     halo_start(0)
     for (here, _), copy in zip(sides, near_copies()):
         pl.when(here)(copy.start)
-    send_all(info, info_all, 0)
+    gather_start(info, info_all, 0)
     info_all[pl.ds(me, 1)] = info[...][None]
 
     local[...] = jnp.zeros_like(local)
+    loads[5].wait()
+    loads[6].wait()
     for i in range(rows):
         for j in range(cols):
             p = i * cols + j
             tiles = [a_ref[i, j, :, s * blk : (s + 1) * blk] for s in range(5)]
-            names = [cols_ref[i, j, s] for s in range(5)]
+            names = [cols_ref[j, i, s] for s in range(5)]
             for d, (di, dj) in enumerate(((0, 0), (-1, 0), (1, 0), (0, -1), (0, 1))):
                 e = (i + 1 + di) * (cols + 2) + j + 1 + dj
                 tile = tiles[0] * (names[0] == e).astype(jnp.float32)
@@ -203,25 +270,32 @@
         for i in range(rows):
             yield 3, i, 2 * cols + rows + i, i * cols + cols - 1
 
-    def operate(v, k):
+    def operate(v, k, beside=lambda: None):
         inner = mm(local[...], stacked(v))
+        beside()
         parts = [inner[p * blk : (p + 1) * blk] for p in range(count)]
         halo_wait(k)
         for side, at, e, p in places():
             parts[p] = parts[p] + mm(edge[e], stacked(halos[side][k, at]))
         return jnp.concatenate(parts, axis=0)
 
-    own_n = n_ref[...]
+    own_n = nulls[...]
     own_hi, own_lo = cut(own_n)
     own_cat = jnp.concatenate([own_hi, own_hi, own_lo], axis=1)
 
     def restrict(v, k):
         g = mm(own_cat, stacked(v))
         coarse[k] = g
-        send_all(coarse.at[k], coarse_all.at[k], 1 + k)
+        gather_start(mine(k), theirs_all(k), 1 + k)
         coarse_all[k, pl.ds(me, 1)] = g[None]
 
-    r = b - operate(first, 0)
+    def mine(k):
+        return coarse.at[k, 0:modes]
+
+    def theirs_all(k):
+        return coarse_all.at[k, :, 0:modes]
+
+    r = b - operate(first, 0, lambda: gather_pass(info, info_all, 0))
     restrict(r, 0)
 
     for side, (here, _) in enumerate(sides):
@@ -259,7 +333,8 @@
         mm_t(eye, part).astype(jnp.bfloat16) for part in cut(at_rows(0, own_n))
     )
 
-    wait_all(info_all, all_recv.at[0])
+    gather_pass(mine(0), theirs_all(0), 1)
+    gather_end(info_all, 0)
     inv_all = info_all[...].reshape(coarse_rows, width)
     ids = [me] + [
         jnp.clip(px, 0, nx - 1) * ny + jnp.clip(py, 0, ny - 1) for _, (px, py) in sides
@@ -286,7 +361,7 @@
     solve_cut = cut(mm_t(picked, order, precision=highest))
 
     def correct(k):
-        wait_all(coarse_all.at[k], all_recv.at[1 + k])
+        gather_end(theirs_all(k), 1 + k)
         h = mm3(solve_cut, coarse_all[k].reshape(coarse_rows, cases))
         return mm3(prolong_cut, h), mm3(spread_cut, h)
 
@@ -304,6 +379,7 @@
     s, r = relax(r, 2)
     precond = precond + s
     restrict(r, 1)
+    gather_pass(mine(1), theirs_all(1), 2)
     up_by, down_by = correct(1)
     precond = precond + up_by
     r = r - down_by
@@ -319,23 +395,33 @@
         ],
         axis=0,
     )
-    send_all(sums, sums_all, 3)
+
+    def share(j, carry):
+        peer = lax.rem(me + j, n)
+        pltpu.make_async_remote_copy(
+            src_ref=sums.at[0:2], dst_ref=sums_all.at[me, 0:2], send_sem=sum_send, recv_sem=sum_recv,
+            device_id=(peer // ny, lax.rem(peer, ny)), device_id_type=pl.DeviceIdType.MESH,
+        ).start()
+        return carry
+
+    lax.fori_loop(1, n, share, 0)
     sums_all[pl.ds(me, 1)] = sums[...][None]
-    wait_all(sums_all, all_recv.at[3])
-    total = jnp.sum(sums_all[...], axis=0)
-    alpha = total[0:1] / total[1:2]
-    sol_ref[...] = (alpha * precond).reshape(rows, cols, blk, cases)
-    res_ref[...] = (b - alpha * image).reshape(rows, cols, blk, cases)
+    precond_ref[...] = precond.reshape(rows, cols, blk, cases)
+    image_ref[...] = image.reshape(rows, cols, blk, cases)
+    pairs = sums_all.at[:, 0:2]
+    wait_many(pairs, n - 1, sum_recv)
+    total = jnp.sum(sums_all[:, 0:2], axis=0)
+    alpha_ref[...] = total[0:1] / total[1:2]
 
     for k in range(4):
         for (here, _), copy in zip(sides, halo_copies(k)):
             pl.when(here)(copy.wait_send)
     for (here, _), copy in zip(sides, near_copies()):
         pl.when(here)(copy.wait_send)
-    wait_all(info_all, all_send.at[0])
-    wait_all(coarse_all.at[0], all_send.at[1])
-    wait_all(coarse_all.at[1], all_send.at[2])
-    wait_all(sums_all, all_send.at[3])
+    gather_sent(info, info_all, 0)
+    gather_sent(mine(0), theirs_all(0), 1)
+    gather_sent(mine(1), theirs_all(1), 2)
+    wait_many(pairs, n - 1, sum_send)
 
 
 def fused(
@@ -347,19 +433,29 @@
     modes = near_null.shape[2] // blk
     n = nx * ny
     width = -(-coarse_inverse.shape[1] // 128) * 128
-    near = jnp.transpose(near_null.reshape(count, modes, blk), (1, 0, 2)).reshape(modes, -1)
-    near = jnp.pad(near, ((0, 8 - modes), (0, 0)))
-    blocks = smoother_blocks.reshape(count, blk, blk)
+    block_cols = jnp.transpose(block_cols, (1, 0, 2))
+    smoother_blocks = jnp.transpose(smoother_blocks, (1, 0, 2))
+    near_null = jnp.transpose(near_null, (1, 0, 2))
     vmem = pl.BlockSpec(memory_space=pltpu.VMEM)
-    smem = pl.BlockSpec(memory_space=pltpu.SMEM)
+    hbm = pl.BlockSpec(memory_space=pltpu.HBM)
     f32, bf16 = jnp.float32, jnp.bfloat16
     shape = jax.ShapeDtypeStruct(load_cases.shape, f32)
-    return pl.pallas_call(
+    precond, image, alpha = pl.pallas_call(
         functools.partial(step_kernel, nx, ny, modes),
-        out_shape=(shape, shape),
-        in_specs=[vmem, vmem, smem, vmem, vmem, smem, vmem],
-        out_specs=(vmem, vmem),
+        out_shape=(shape, shape, jax.ShapeDtypeStruct((1, cases), f32)),
+        in_specs=[hbm] * 7,
+        out_specs=(vmem, vmem, vmem),
         scratch_shapes=[
+            pltpu.VMEM(load_cases.shape, f32),
+            pltpu.VMEM(matrix_tiles.shape, f32),
+            pltpu.SMEM(block_cols.shape, jnp.int32),
+            pltpu.VMEM(smoother_blocks.shape, f32),
+            pltpu.VMEM(near_null.shape, f32),
+            pltpu.SMEM(coarse_map.shape, jnp.int32),
+            pltpu.VMEM(coarse_inverse.shape, f32),
+            pltpu.SemaphoreType.DMA((7,)),
+            pltpu.VMEM((count, 2, blk, 128), f32),
+            pltpu.VMEM((8, count * blk), f32),
             pltpu.VMEM((4, rows, cols, blk, cases), f32),
             pltpu.VMEM((4, cols, blk, cases), f32),
             pltpu.VMEM((4, cols, blk, cases), f32),
@@ -379,13 +475,22 @@
             pltpu.SemaphoreType.DMA((4, 4)),
             pltpu.SemaphoreType.DMA((4,)),
             pltpu.SemaphoreType.DMA((4,)),
-            pltpu.SemaphoreType.DMA((4,)),
-            pltpu.SemaphoreType.DMA((4,)),
+            pltpu.SemaphoreType.DMA((3, ny)),
+            pltpu.SemaphoreType.DMA((3, ny)),
+            pltpu.SemaphoreType.DMA((3,)),
+            pltpu.SemaphoreType.DMA((3,)),
+            pltpu.SemaphoreType.DMA,
+            pltpu.SemaphoreType.DMA,
         ],
         compiler_params=pltpu.CompilerParams(
             collective_id=0, has_side_effects=True, vmem_limit_bytes=60 * 2**20
         ),
-    )(load_cases, matrix_tiles, block_cols, blocks, near, coarse_map, coarse_inverse)
+    )(
+        load_cases, matrix_tiles, block_cols, smoother_blocks, near_null, coarse_map,
+        coarse_inverse,
+    )
+    alpha = alpha.reshape(1, 1, 1, cases)
+    return alpha * precond, load_cases - alpha * image
 
 
 def per_device(

time: 53.6 us -> 50.3 us (0.938)
  local copies, waits for them, and re-layouts: 6.04 us -> 0.65 us
  other arithmetic: 0 us -> 1.8 us
    unnamed x9 -> x4, local copies, waits for them, and re-layouts: 4.43 us -> 0.65 us
    sub x0 -> x1, other arithmetic: none -> 1.8 us  [fused(): return (alpha * precond, load_cases - alpha * image)]
    reshape x3 -> x0, local copies, waits for them, and re-layouts: 0.99 us -> none  [the longest x1 0.84 us: fused(): blocks = smoother_blocks.reshape(count, blk, blk)]
    pad x1 -> x0, local copies, waits for them, and re-layouts: 0.61 us -> none  [fused(): near = jnp.pad(near, ((0, 8 - modes), (0, 0)))]
where the time goes in v2:
time: 50.3 us; the launch traced here: 50.1 us
  Pallas kernels  47 us (93%)
  other arithmetic  1.8 us (4%)
  between operations  0.66 us (1%)
  local copies, waits for them, and re-layouts  0.65 us (1%)
    pallas_call x1, Pallas kernels, fused(): pl.pallas_call(functools.partial(step_kernel, nx, ny, modes), out_shape=(...  47 us
    sub x1, other arithmetic, fused(): return (alpha * precond, load_cases - alpha * image)  1.8 us

profile of v2, /device:TPU:0, one launch (start us, length us, event | category | flops | bytes accessed | tf_op | source)
XLA Modules:
  0.0 50.1 jit_solution(7857296993853833571)
XLA Ops:
  0.6 0.0 copy-start
  0.6 47.0 %shard_map.86 = (f32[2,3,64,128]{3,2,1,0:T(8,128)}, f32[2,3,64,128]{3,2,1,0:T(8,128)}, f32[1,128]{1,0:T(1,128)}) custom-call(f32[2,3,64,128]{3,2,1,0:T(8,128)} %b_hbm.1, f32[2,3,64,320]{3,2,1,0:T(8,128)} %a_hbm.1, s32[3,2,5]{2,1,0:T(2,128)} %bitcast.6, f32[3,2,4096]{2,1,0:T(2,128)} %bitcast.4, f32[3,2,384]{2,1,0:T(2,128)} %bitcast.5, s32[2,3]{1,0:T(2,128)} %map_hbm.1, ...), custom_call_target="tpu_custom_call" | custom-call | tf_op jit(solution)/shard_map/pallas_call | solution.py:443
  47.7 0.0 copy-start.1
  47.7 0.0 copy-done
  47.7 0.6 %copy-done.1 = f32[1,128]{1,0:T(1,128)S(1)} copy-done((f32[1,128]{1,0:T(1,128)S(1)}, f32[1,128]{1,0:T(1,128)}, u32[]{:S(2)}) %copy-start.1) | copy-done | bytes 536
  48.3 1.8 %multiply_subtract_fusion = (f32[2,3,64,128]{3,2,1,0:T(8,128)}, f32[2,3,64,128]{3,2,1,0:T(8,128)}) fusion(f32[2,3,64,128]{3,2,1,0:T(8,128)S(1)} %copy-done, f32[2,3,64,128]{3,2,1,0:T(8,128)} %get-tuple-element.7, f32[128]{0:T(128)S(1)} %bitcast.7, f32[2,3,64,128]{3,2,1,0:T(8,128)} %get-tuple-element.6), kind=kLoop, calls=%fused_computation | loop fusion | flops 147456 | bytes 983552 | tf_op jit(solution)/shard_map/sub | solution.py:493
Async XLA Ops:
  0.6 47.0 %copy-start = (f32[2,3,64,128]{3,2,1,0:T(8,128)S(1)}, f32[2,3,64,128]{3,2,1,0:T(8,128)}, u32[]{:S(2)}) copy-start(f32[2,3,64,128]{3,2,1,0:T(8,128)} %b_hbm.1) | copy-start | bytes 589828
  47.7 0.7 %copy-start.1 = (f32[1,128]{1,0:T(1,128)S(1)}, f32[1,128]{1,0:T(1,128)}, u32[]{:S(2)}) copy-start(f32[1,128]{1,0:T(1,128)} %get-tuple-element.5) | copy-start | bytes 1540

commit v3 on v2

--- a/solution.py
+++ b/solution.py
@@ -169,10 +169,9 @@
         for (here, _), copy in zip(sides, halo_copies(k)):
             pl.when(here)(copy.start)
 
-    def halo_wait(k):
-        for side, (here, _) in enumerate(sides):
-            buf = halos[side].at[k]
-            pl.when(here)(pltpu.make_async_copy(buf, buf, halo_recv.at[k, side]).wait)
+    def halo_wait(k, side):
+        buf = halos[side].at[k]
+        pl.when(sides[side][0])(pltpu.make_async_copy(buf, buf, halo_recv.at[k, side]).wait)
 
     def near_copies():
         return [
@@ -228,13 +227,6 @@
     info[...] = jnp.zeros_like(info)
     info[0:modes, 0 : inv_ref.shape[1]] = inv_ref[...]
     info[modes : modes + 1, :] = jnp.full((1, width), map_ref[0, 0].astype(jnp.float32))
-
-    pl.semaphore_wait(barrier, n - 1)
-    halo_start(0)
-    for (here, _), copy in zip(sides, near_copies()):
-        pl.when(here)(copy.start)
-    gather_start(info, info_all, 0)
-    info_all[pl.ds(me, 1)] = info[...][None]
 
     local[...] = jnp.zeros_like(local)
     loads[5].wait()
@@ -260,6 +252,13 @@
                     at = (0, j, cols + j, 2 * cols + i, 2 * cols + rows + i)[d]
                     edge[at] = jnp.concatenate([hi, hi, lo], axis=1)
 
+    pl.semaphore_wait(barrier, n - 1)
+    halo_start(0)
+    for (here, _), copy in zip(sides, near_copies()):
+        pl.when(here)(copy.start)
+    gather_start(info, info_all, 0)
+    info_all[pl.ds(me, 1)] = info[...][None]
+
     def places():
         for j in range(cols):
             yield 0, j, j, j
@@ -270,13 +269,14 @@
         for i in range(rows):
             yield 3, i, 2 * cols + rows + i, i * cols + cols - 1
 
-    def operate(v, k, beside=lambda: None):
+    def operate(v, k):
         inner = mm(local[...], stacked(v))
-        beside()
         parts = [inner[p * blk : (p + 1) * blk] for p in range(count)]
-        halo_wait(k)
-        for side, at, e, p in places():
-            parts[p] = parts[p] + mm(edge[e], stacked(halos[side][k, at]))
+        for side in (2, 3, 0, 1):
+            halo_wait(k, side)
+            for at_side, at, e, p in places():
+                if at_side == side:
+                    parts[p] = parts[p] + mm(edge[e], stacked(halos[side][k, at]))
         return jnp.concatenate(parts, axis=0)
 
     own_n = nulls[...]
@@ -295,8 +295,9 @@
     def theirs_all(k):
         return coarse_all.at[k, :, 0:modes]
 
-    r = b - operate(first, 0, lambda: gather_pass(info, info_all, 0))
+    r = b - operate(first, 0)
     restrict(r, 0)
+    gather_pass(info, info_all, 0)
 
     for side, (here, _) in enumerate(sides):
         buf = near.at[side]
@@ -324,7 +325,7 @@
         q = facing[side](at)
         block = theirs[side][:, q * blk : (q + 1) * blk]
         parts[p] = parts[p] + mm_t(edge[e], across(at_rows(1 + side, block)))
-    spread_cut = cut(jnp.concatenate(parts, axis=0))
+    spread = jnp.concatenate(parts, axis=0)
     eye = (
         lax.broadcasted_iota(jnp.int32, (size, size), 0)
         == lax.broadcasted_iota(jnp.int32, (size, size), 1)
@@ -358,12 +359,14 @@
     labels = jnp.broadcast_to(info_all[...][:, modes : modes + 1, :], (n, 8, width))
     order = jnp.where(lane3 == labels * float(modes) + row3.astype(jnp.float32), 1.0, 0.0)
     order = jnp.where(row3 < modes, order, 0.0).reshape(coarse_rows, width)
-    solve_cut = cut(mm_t(picked, order, precision=highest))
+    solve = mm_t(picked, order, precision=highest)
+    solve_cut = cut(solve)
+    spread_cut = cut(mm3(cut(spread), solve))
 
     def correct(k):
         gather_end(theirs_all(k), 1 + k)
-        h = mm3(solve_cut, coarse_all[k].reshape(coarse_rows, cases))
-        return mm3(prolong_cut, h), mm3(spread_cut, h)
+        g = coarse_all[k].reshape(coarse_rows, cases)
+        return mm3(prolong_cut, mm3(solve_cut, g)), mm3(spread_cut, g)
 
     def relax(v, k):
         s = smooth(v)
@@ -422,6 +425,34 @@
     gather_sent(mine(0), theirs_all(0), 1)
     gather_sent(mine(1), theirs_all(1), 2)
     wait_many(pairs, n - 1, sum_send)
+
+
+def finish_kernel(b_ref, p_ref, i_ref, alpha_ref, sol_ref, res_ref, held, scale, sems, scale_sem):
+    rows = b_ref.shape[0]
+    first = pltpu.make_async_copy(alpha_ref, scale, scale_sem)
+    first.start()
+
+    def move(k, i):
+        ref = (p_ref, i_ref, b_ref, sol_ref, res_ref)[k]
+        ends = (ref.at[i], held.at[k, i])
+        return pltpu.make_async_copy(*(ends if k < 3 else ends[::-1]), sems.at[k, i])
+
+    for i in range(rows):
+        for k in range(3):
+            move(k, i).start()
+    first.wait()
+    alpha = scale[...].reshape(1, 1, -1)
+    for i in range(rows):
+        move(0, i).wait()
+        held[3, i] = alpha * held[0, i]
+        move(3, i).start()
+        move(1, i).wait()
+        move(2, i).wait()
+        held[4, i] = held[2, i] - alpha * held[1, i]
+        move(4, i).start()
+    for i in range(rows):
+        move(3, i).wait()
+        move(4, i).wait()
 
 
 def fused(
@@ -489,8 +520,19 @@
         load_cases, matrix_tiles, block_cols, smoother_blocks, near_null, coarse_map,
         coarse_inverse,
     )
-    alpha = alpha.reshape(1, 1, 1, cases)
-    return alpha * precond, load_cases - alpha * image
+    return pl.pallas_call(
+        finish_kernel,
+        out_shape=(shape, shape),
+        in_specs=[hbm, hbm, hbm, hbm],
+        out_specs=(hbm, hbm),
+        scratch_shapes=[
+            pltpu.VMEM((5,) + load_cases.shape, f32),
+            pltpu.VMEM((1, cases), f32),
+            pltpu.SemaphoreType.DMA((5, rows)),
+            pltpu.SemaphoreType.DMA,
+        ],
+        compiler_params=pltpu.CompilerParams(vmem_limit_bytes=60 * 2**20),
+    )(load_cases, precond, image, alpha)
 
 
 def per_device(

time: 50.3 us -> 49.3 us (0.980)
  other arithmetic: 1.8 us -> 0 us
  Pallas kernels: 47 us -> 48.4 us
  local copies, waits for them, and re-layouts: 0.65 us -> 0 us
    pallas_call x0 -> x1, Pallas kernels: none -> 1.88 us  [fused(): pl.pallas_call(finish_kernel, out_shape=(shape, shape), in_specs=[hbm, hb...]
    sub x1 -> x0, other arithmetic: 1.8 us -> none  [fused(): return (alpha * precond, load_cases - alpha * image)]
    unnamed x4 -> x0, local copies, waits for them, and re-layouts: 0.65 us -> none
where the time goes in v3:
time: 49.3 us; the launch traced here: 49.1 us
  Pallas kernels  48.4 us (98%)
  between operations  0.64 us (1%)
    pallas_call x1, Pallas kernels, fused(): pl.pallas_call(functools.partial(step_kernel, nx, ny, modes), out_shape=(...  46.6 us
    pallas_call x1, Pallas kernels, fused(): pl.pallas_call(finish_kernel, out_shape=(shape, shape), in_specs=[hbm, hb...  1.88 us

profile of v3, /device:TPU:0, one launch (start us, length us, event | category | flops | bytes accessed | tf_op | source)
XLA Modules:
  0.0 49.1 jit_solution(34723314608553108)
XLA Ops:
  0.6 46.6 %shard_map.86 = (f32[2,3,64,128]{3,2,1,0:T(8,128)}, f32[2,3,64,128]{3,2,1,0:T(8,128)}, f32[1,128]{1,0:T(1,128)}) custom-call(f32[2,3,64,128]{3,2,1,0:T(8,128)} %b_ref.1, f32[2,3,64,320]{3,2,1,0:T(8,128)} %a_hbm.1, s32[3,2,5]{2,1,0:T(2,128)} %bitcast.5, f32[3,2,4096]{2,1,0:T(2,128)} %bitcast.3, f32[3,2,384]{2,1,0:T(2,128)} %bitcast.4, s32[2,3]{1,0:T(2,128)} %map_hbm.1, ...), custom_call_target="tpu_custom_call" | custom-call | tf_op jit(solution)/shard_map/pallas_call | solution.py:474
  47.2 1.9 %shard_map.87 = (f32[2,3,64,128]{3,2,1,0:T(8,128)}, f32[2,3,64,128]{3,2,1,0:T(8,128)}) custom-call(f32[2,3,64,128]{3,2,1,0:T(8,128)} %b_ref.1, f32[2,3,64,128]{3,2,1,0:T(8,128)} %get-tuple-element.5.p_ref, f32[2,3,64,128]{3,2,1,0:T(8,128)} %get-tuple-element.6.i_ref, f32[1,128]{1,0:T(1,128)} %get-tuple-element.7.alpha_ref), custom_call_target="tpu_custom_call" | custom-call | tf_op jit(solution)/shard_map/pallas_call | solution.py:523

commit v4 on v3

--- a/solution.py
+++ b/solution.py
@@ -79,6 +79,8 @@
     halos = (up, down, left, right)
 
     coarse_all[...] = jnp.zeros_like(coarse_all)
+    info_all[...] = jnp.zeros_like(info_all)
+    told, told_all = info.at[0 : modes + 1], info_all.at[:, 0 : modes + 1]
     barrier = pltpu.get_barrier_semaphore()
 
     def greet(j, carry):
@@ -256,7 +258,7 @@
     halo_start(0)
     for (here, _), copy in zip(sides, near_copies()):
         pl.when(here)(copy.start)
-    gather_start(info, info_all, 0)
+    gather_start(told, told_all, 0)
     info_all[pl.ds(me, 1)] = info[...][None]
 
     def places():
@@ -297,7 +299,7 @@
 
     r = b - operate(first, 0)
     restrict(r, 0)
-    gather_pass(info, info_all, 0)
+    gather_pass(told, told_all, 0)
 
     for side, (here, _) in enumerate(sides):
         buf = near.at[side]
@@ -335,7 +337,7 @@
     )
 
     gather_pass(mine(0), theirs_all(0), 1)
-    gather_end(info_all, 0)
+    gather_end(told_all, 0)
     inv_all = info_all[...].reshape(coarse_rows, width)
     ids = [me] + [
         jnp.clip(px, 0, nx - 1) * ny + jnp.clip(py, 0, ny - 1) for _, (px, py) in sides
@@ -421,7 +423,7 @@
             pl.when(here)(copy.wait_send)
     for (here, _), copy in zip(sides, near_copies()):
         pl.when(here)(copy.wait_send)
-    gather_sent(info, info_all, 0)
+    gather_sent(told, told_all, 0)
     gather_sent(mine(0), theirs_all(0), 1)
     gather_sent(mine(1), theirs_all(1), 2)
     wait_many(pairs, n - 1, sum_send)

time: 49.3 us -> 49.2 us (level)
  no operation moved by 1% of the time
where the time goes in v4:
time: 49.2 us; the launch traced here: 49.1 us
  Pallas kernels  48.4 us (98%)
  between operations  0.64 us (1%)
    pallas_call x1, Pallas kernels, fused(): pl.pallas_call(functools.partial(step_kernel, nx, ny, modes), out_shape=(...  46.5 us
    pallas_call x1, Pallas kernels, fused(): pl.pallas_call(finish_kernel, out_shape=(shape, shape), in_specs=[hbm, hb...  1.88 us

profile of v4, /device:TPU:0, one launch (start us, length us, event | category | flops | bytes accessed | tf_op | source)
XLA Modules:
  0.0 49.1 jit_solution(7687894247168030777)
XLA Ops:
  0.6 46.5 %shard_map.86 = (f32[2,3,64,128]{3,2,1,0:T(8,128)}, f32[2,3,64,128]{3,2,1,0:T(8,128)}, f32[1,128]{1,0:T(1,128)}) custom-call(f32[2,3,64,128]{3,2,1,0:T(8,128)} %b_ref.1, f32[2,3,64,320]{3,2,1,0:T(8,128)} %a_hbm.1, s32[3,2,5]{2,1,0:T(2,128)} %bitcast.5, f32[3,2,4096]{2,1,0:T(2,128)} %bitcast.3, f32[3,2,384]{2,1,0:T(2,128)} %bitcast.4, s32[2,3]{1,0:T(2,128)} %map_hbm.1, ...), custom_call_target="tpu_custom_call" | custom-call | tf_op jit(solution)/shard_map/pallas_call | solution.py:476
  47.2 1.9 %shard_map.87 = (f32[2,3,64,128]{3,2,1,0:T(8,128)}, f32[2,3,64,128]{3,2,1,0:T(8,128)}) custom-call(f32[2,3,64,128]{3,2,1,0:T(8,128)} %b_ref.1, f32[2,3,64,128]{3,2,1,0:T(8,128)} %get-tuple-element.5.p_ref, f32[2,3,64,128]{3,2,1,0:T(8,128)} %get-tuple-element.6.i_ref, f32[1,128]{1,0:T(1,128)} %get-tuple-element.7.alpha_ref), custom_call_target="tpu_custom_call" | custom-call | tf_op jit(solution)/shard_map/pallas_call | solution.py:525
